TPU v7x, 128 devices: a whole 4x4x4 slice. The times are simulated.
128 devices in a mesh: mgroup: 16 (over y_hi, z, core), msub: 8 (over x, y_lo).
Axes of the slice: x: 4, y: 4 (y_hi: 2, y_lo: 2; y = y_hi * 2 + y_lo), z: 4, core: 2. Of those that a mesh axis runs over, the one named last changes fastest.
Arguments:
- in_modes: int32 [128, 2], P(('mgroup', 'msub')), may hold values from 0 to 31
- back_first: bfloat16 [128, 1024, 2048], P(('mgroup', 'msub')), may hold values from -192 to 192
- back_second: bfloat16 [128, 1024, 2048], P(('mgroup', 'msub')), may hold values from -512 to 512
Outputs:
- mask_first: float32 [1024, 2048], P(('mgroup', 'msub'))
- mask_second: float32 [1024, 2048], P(('mgroup', 'msub'))
Inputs may be any that keep to these rules, and one draw needn't show every extreme that they name: `in_modes`: each row holds a mode's row order and column order.
All inputs are finite; a program needn't handle non-finite values.
Results may differ from a plain program's by a relative error of at most 0.013.
Values may be sent and summed in bfloat16 or wider, within the bound.
No kernel may reach another device: no remote copies, remote signals or barrier semaphores. Data moves between devices by JAX's collectives and lax.ppermute only.
A program may use at most 128 MiB of HBM per device.

v0:
```python
import math

import jax
import jax.numpy as jnp
from jax import lax
from jax.sharding import PartitionSpec as P

ORDERS = 32


span_width = 24.0


def grid_points(cells):
    index = jnp.arange(cells, dtype=jnp.float32)
    return (index - cells / 2 + 0.5) * (span_width / cells)


def hermite_table(points):
    before = jnp.zeros_like(points)
    current = math.pi ** (-0.25) * jnp.exp(-0.5 * points * points)
    collected = []
    for order in range(ORDERS):
        collected.append(current)
        following = (
            math.sqrt(2.0 / (order + 1)) * points * current
            - math.sqrt(order / (order + 1.0)) * before
        )
        before, current = (current, following)
    return jnp.stack(collected, axis=0)


def chirp_parts(cells):
    index = jnp.arange(cells, dtype=jnp.int32)
    offset = index[:, None] - index[None, :]
    square = offset * offset % (2 * cells)
    phase = square.astype(jnp.float32) * (math.pi / cells)
    factor = cells ** (-0.5)
    return (
        (jnp.cos(phase) * factor).astype(jnp.bfloat16),
        (jnp.sin(phase) * factor).astype(jnp.bfloat16),
    )


def soften(intersection):
    half = intersection.shape[-1] // 2
    real_part = intersection[..., :half]
    imag_part = intersection[..., half:]
    denom = jnp.sqrt(real_part * real_part + imag_part * imag_part + 1.0)
    return intersection / jnp.concatenate([denom, denom], axis=-1)


def pick_funcs(orders, herm_table):
    one_hot = (orders[:, None] == jnp.arange(herm_table.shape[0], dtype=jnp.int32)[None, :]).astype(
        jnp.float32
    )
    return jnp.dot(one_hot, herm_table, precision=lax.Precision.HIGHEST)


def intersection_first(back_rows, field_rows):
    widened = field_rows.astype(jnp.float32)
    tiled = jnp.concatenate([widened, widened], axis=2)
    return jnp.sum(back_rows.astype(jnp.float32) * tiled, axis=0)


def propagate_rows(mask_rows, field_rows, big_chirp):
    widened = field_rows.astype(jnp.float32)
    tiled = jnp.concatenate([widened, widened], axis=2)
    applied = (mask_rows.astype(jnp.float32)[None] * tiled).astype(jnp.bfloat16)
    return jnp.einsum("mrk,kc->mrc", applied, big_chirp, preferred_element_type=jnp.float32).astype(
        jnp.bfloat16
    )


def intersection_conj(back_rows, arrived, cells):
    back_real = back_rows[:, :, :cells]
    back_imag = back_rows[:, :, cells:]
    arr_real = arrived[:, :, :cells]
    arr_imag = arrived[:, :, cells:]
    real_part = jnp.sum(back_real * arr_real + back_imag * arr_imag, axis=0)
    imag_part = jnp.sum(back_imag * arr_real - back_real * arr_imag, axis=0)
    return jnp.concatenate([real_part, imag_part], axis=1)


def body(in_modes, back_first, back_second):
    mode_dev = in_modes.shape[0]
    cells = back_first.shape[1]
    groups_sub = lax.axis_size("msub")
    devices_all = lax.axis_size("mgroup") * groups_sub
    strip_rows = cells // devices_all
    scale_all = float(mode_dev * devices_all) ** (-0.5)
    herm_table = hermite_table(grid_points(cells))
    row_funcs = pick_funcs(in_modes[:, 0], herm_table)
    col_funcs = pick_funcs(in_modes[:, 1], herm_table)
    fields = (row_funcs[:, :, None] * col_funcs[:, None, :]).astype(jnp.bfloat16)
    chirp_real, chirp_imag = chirp_parts(cells)
    big_chirp = jnp.concatenate(
        [
            jnp.concatenate([chirp_real, chirp_imag], axis=1),
            jnp.concatenate([-chirp_imag, chirp_real], axis=1),
        ],
        axis=0,
    )
    back_rows = back_first
    summed = lax.psum(intersection_first(back_rows, fields), ("mgroup", "msub"))
    full_mask = soften(summed * scale_all)
    own_start = lax.axis_index(("mgroup", "msub")) * strip_rows
    mask_first = lax.dynamic_slice_in_dim(full_mask, own_start, strip_rows, 0)
    spread = propagate_rows(full_mask.astype(jnp.bfloat16), fields, big_chirp)
    rotated = jnp.concatenate([-spread[:, :, cells:], spread[:, :, :cells]], axis=2)
    arrived = jnp.einsum("rk,mkc->mrc", chirp_real, spread, preferred_element_type=jnp.float32)
    arrived = arrived + jnp.einsum(
        "rk,mkc->mrc", chirp_imag, rotated, preferred_element_type=jnp.float32
    )
    back_rows = back_second.astype(jnp.float32)
    summed_two = lax.psum_scatter(
        intersection_conj(back_rows, arrived, cells),
        ("mgroup", "msub"),
        scatter_dimension=0,
        tiled=True,
    )
    mask_second = soften(summed_two * scale_all)
    return (mask_first, mask_second)


def solution(mesh):
    placed = (
        P(("mgroup", "msub"), None),
        P(("mgroup", "msub"), None, None),
        P(("mgroup", "msub"), None, None),
    )
    return jax.shard_map(
        body,
        mesh=mesh,
        in_specs=placed,
        out_specs=(P(("mgroup", "msub"), None), P(("mgroup", "msub"), None)),
        check_vma=False,
    )
```

profile of v0, /device:TPU:0, one launch (start us, length us, event | category | flops | bytes accessed | tf_op | source)
XLA Modules:
  0.0 939.3 jit_solution(4741200665334392531)
XLA Ops:
  9.0 1.3 fusion.51
  10.5 0.8 fusion.29
  11.3 0.8 fusion.31
  12.4 5.6 multiply_bitcast_fusion
  18.2 6.3 copy.14
  24.5 6.8 convert_element_type.80
  31.6 16.7 %fusion.24 = bf16[1024,1024]{1,0:T(8,128)(2,1)} fusion(), kind=kLoop, calls=%fused_computation.41 | loop fusion | flops 20971520 | bytes 2097152 | tf_op jit(solution)/shard_map/neg | solution.py:100
  48.3 18.1 %multiply_convert_fusion.2 = (bf16[1024,1024]{1,0:T(8,128)(2,1)}, bf16[1024,1024]{1,0:T(8,128)(2,1)}) fusion(), kind=kLoop, calls=%fused_computation.33 | loop fusion | flops 19922944 | bytes 4194304 | tf_op jit(solution)/shard_map/convert_element_type | solution.py:41
  66.4 116.1 %all-reduce.2.cloned.1.call-done = f32[1024,2048]{1,0:T(8,128)} async-done(((f32[1024,2048]{1,0:T(8,128)}), f32[1024,2048]{1,0:T(8,128)}) %all-reduce.2.cloned.1.call-update) | async-done | bytes 8388624 | tf_op jit(solution)/shard_map/psum | solution.py:105
  182.5 5.2 broadcast_multiply_fusion
  187.7 1.6 fusion.13
  189.3 1.8 copy-done
  191.1 5.0 maximum_divide_fusion
  196.0 16.5 %fusion.21 = bf16[1024,2048]{1,0:T(8,128)(2,1)} fusion(bf16[1024,1024]{1,0:T(8,128)(2,1)} %get-tuple-element.47, bf16[1024,1024]{1,0:T(8,128)(2,1)} %fusion.24, bf16[1024,1024]{1,0:T(8,128)(2,1)} %get-tuple-element.46, bf16[1024,1024]{1,0:T(8,128)(2,1)S(1)} %multiply_convert_fusion.4, f32[1024,2048]{1,0:T(8,128)} %maximum_divide_fusion), kind=kOutput, calls=%fused_computation.39 | convolution fusion | flops 8642363392 | bytes 20971520 | tf_op jit(solution)/shard_map/mrk,kc->mrc/dot_general | solution.py:70
  212.6 2.6 slice_negate_fusion
  215.3 18.9 %fusion.17 = f32[2048,1024]{1,0:T(8,128)S(1)} fusion(bf16[1,1024,1024]{2,1,0:T(8,128)(2,1)S(1)} %get-tuple-element.11, bf16[1,1024,1024]{2,1,0:T(8,128)(2,1)S(1)} %get-tuple-element.10), kind=kOutput, calls=%fused_computation.28 | convolution fusion | flops 4321181696 | bytes 12582912 | tf_op jit(solution)/shard_map/rk,mkc->mrc/dot_general | solution.py:112
  234.2 22.1 %add_bitcast_fusion = f32[1,1024,2048]{1,2,0:T(8,128)S(1)} fusion(f32[2048,1024]{1,0:T(8,128)S(1)} %fusion.17, bf16[1024,2048]{1,0:T(8,128)(2,1)S(1)} %copy-done.1), kind=kOutput, calls=%fused_computation.10 | convolution fusion | flops 4314890240 | bytes 20971520 | tf_op jit(solution)/shard_map/rk,mkc->mrc/dot_general | solution.py:111
  256.3 2.0 add_bitcast_fusion.1
  258.3 4.1 pad_maximum_fusion
  262.4 9.3 copy.16
  271.7 1.5 constant_dynamic-slice_fusion
  273.2 656.6 %reduce-scatter.4.cloned.1.call-done = f32[8,2048]{1,0:T(8,128)} async-done(((f32[1024,2048]{1,0:T(8,128)}), f32[8,2048]{1,0:T(8,128)}) %reduce-scatter.4.cloned.1.call-update) | async-done | bytes 65552 | tf_op jit(solution)/shard_map/reduce_scatter | solution.py:116
  929.9 0.8 broadcast_multiply_fusion.1
  930.7 1.5 maximum_divide_fusion.1
  (32 shorter events, 2.7 us)
Async XLA Ops:
  7.2 175.3 %all-reduce.2.cloned.1.call-start = ((), (), s32[]{:S(2)}) async-start(), calls=%async_computation.1 | async-start | bytes 16777216 | tf_op jit(solution)/shard_map/psum | solution.py:105
  18.1 911.7 %reduce-scatter.4.cloned.1.call-start = ((), (), s32[]{:S(2)}) async-start(), calls=%async_computation.2 | async-start | bytes 8454144 | tf_op jit(solution)/shard_map/reduce_scatter | solution.py:116
  187.7 3.4 copy-start
  212.6 43.7 %slice-start = ((s8[8388608]{0:T(1024)(128)(4,1)}), s8[4194304]{0:T(1024)(128)(4,1)S(1)}, s32[]{:S(2)}) async-start(s8[8388608]{0:T(1024)(128)(4,1)} %bitcast.28), calls=%async_computation.3 | async-start | bytes 8388608
  215.2 19.0 %copy-start.1 = (bf16[1024,2048]{1,0:T(8,128)(2,1)S(1)}, bf16[1024,2048]{1,0:T(8,128)(2,1)}, u32[]{:S(2)}) copy-start(bf16[1024,2048]{1,0:T(8,128)(2,1)} %fusion.21) | copy-start | bytes 12582916
  215.2 41.1 %slice-start.1 = ((s8[8388608]{0:T(1024)(128)(4,1)}), s8[4194304]{0:T(1024)(128)(4,1)S(1)}, s32[]{:S(2)}) async-start(s8[8388608]{0:T(1024)(128)(4,1)} %bitcast.28), calls=%async_computation.4 | async-start | bytes 8388608
Sparse Core Ops, SparseCore 0:
  18.2 164.1 all-reduce.1
  271.9 657.9 reduce-scatter.3
where the time goes:
time: 947 us; the launch traced here: 939 us
  waiting for transfers between devices  773 us (82%)
  other arithmetic  72.5 us (8%)
  matrix products  59.2 us (6%)
  local copies, waits for them, and re-layouts  20.4 us (2%)
  between operations  14.4 us (2%)
    reduce_scatter x1, waiting for transfers between devices, body(): lax.psum_scatter(intersection_conj(back_rows, arrived, cells), ('mgroup',...  657 us
    psum x1, waiting for transfers between devices, body(): summed = lax.psum(intersection_first(back_rows, fields), ('mgroup', 'msub'))  116 us
    dot_general x1, matrix products, body(): jnp.einsum('rk,mkc->mrc', chirp_real, spread, preferred_element_type=jnp....  22.1 us
    dot_general x1, matrix products, body(): jnp.einsum('rk,mkc->mrc', chirp_imag, rotated, preferred_element_type=jnp...  18.9 us
  transfers between devices with their start and end apart: 2, of which 2 were waited for; matrix products, arithmetic and copies ran while one was open for 5% of the time, Pallas kernels for 0%

commit v1 on v0

v1 whole, which is shorter than its diff:
```python
import math

import jax
import jax.numpy as jnp
import numpy as np
from jax import lax
from jax.sharding import Mesh
from jax.sharding import PartitionSpec as P

ORDERS = 32
SPAN = 24.0
AXES = ("yh", "z", "core", "x", "yl")
PEERS = ("yh", "z", "x", "yl")
BF16 = jnp.bfloat16
F32 = jnp.float32


def hermite_table(cells):
    index = np.arange(cells, dtype=np.float32)
    points = ((index - np.float32(cells / 2) + np.float32(0.5)) * np.float32(SPAN / cells)).astype(np.float32)
    before = np.zeros_like(points)
    current = (np.float32(math.pi ** (-0.25)) * np.exp(np.float32(-0.5) * points * points)).astype(np.float32)
    collected = []
    for order in range(ORDERS):
        collected.append(current)
        following = (
            np.float32(math.sqrt(2.0 / (order + 1))) * points * current
            - np.float32(math.sqrt(order / (order + 1.0))) * before
        ).astype(np.float32)
        before, current = (current, following)
    return np.stack(collected, axis=0)


def chirp_halves(cells):
    half = cells // 2
    index = np.arange(half, dtype=np.int64)
    offset = index[:, None] - index[None, :]
    square = offset * offset % (2 * cells)
    phase = square.astype(np.float64) * (math.pi / cells)
    factor = cells ** (-0.5)
    real = (np.cos(phase) * factor).astype(np.float32)
    imag = (np.sin(phase) * factor).astype(np.float32)
    even = offset % 2 == 0
    out = []
    for keep in (even, ~even):
        r = np.where(keep, real, 0.0)
        i = np.where(keep, imag, 0.0)
        out.append((r.astype(jnp.bfloat16), i.astype(jnp.bfloat16)))
    return out


def soften(intersection):
    half = intersection.shape[-1] // 2
    real_part = intersection[..., :half]
    imag_part = intersection[..., half:]
    denom = jnp.sqrt(real_part * real_part + imag_part * imag_part + 1.0)
    return intersection / jnp.concatenate([denom, denom], axis=-1)


def swap_cores(block):
    return lax.ppermute(block, "core", [(0, 1), (1, 0)])


def reduce_rows(product):
    rows, width = product.shape
    core = lax.axis_index("core")
    split = product.reshape(8, 2, 64, width)
    away = lax.dynamic_index_in_dim(split, 1 - core, 1, keepdims=False).astype(BF16)
    keep = lax.dynamic_index_in_dim(split, core, 1, keepdims=False)
    both = (keep.astype(F32) + swap_cores(away).astype(F32)).astype(BF16)
    both = both.reshape(64, rows // 128, width)
    parts = lax.all_to_all(both, PEERS, 0, 0, tiled=True)
    return jnp.sum(parts.astype(F32), axis=0)


def gather_rows(own):
    rows, width = own.shape
    core = lax.axis_index("core")
    mine = lax.all_to_all(jnp.broadcast_to(own[None], (64, rows, width)), PEERS, 0, 0, tiled=True)
    mine = mine.reshape(8, 64, width)
    other = swap_cores(mine)
    first = jnp.where(core == 0, mine, other)
    second = jnp.where(core == 0, other, mine)
    return jnp.stack([first, second], axis=1).reshape(rows * 128, width)


def body(in_modes, back_first, back_second):
    cells = back_first.shape[1]
    half = cells // 2
    scale_all = float(128) ** (-0.5)
    table = jnp.asarray(hermite_table(cells))
    row_func = lax.dynamic_index_in_dim(table, in_modes[0, 0], 0, keepdims=False)
    col_func = lax.dynamic_index_in_dim(table, in_modes[0, 1], 0, keepdims=False)
    field = (row_func[:, None] * col_func[None, :]).astype(BF16).astype(F32)
    tiled = jnp.concatenate([field, field], axis=1)
    summed = reduce_rows(back_first[0].astype(F32) * tiled)
    mask_first = soften(summed * scale_all)
    mask_low = gather_rows(mask_first.astype(BF16))
    (even_r, even_i), (odd_r, odd_i) = jax.tree.map(jnp.asarray, chirp_halves(cells))
    right = []
    left = []
    for r, i in ((even_r, even_i), (odd_r, odd_i)):
        right.append(jnp.block([[r, i], [-i, r]]))
        left.append(jnp.block([[r, -i], [i, r]]))
    applied = (mask_low.astype(F32) * tiled).astype(BF16).astype(F32)
    real, imag = applied[:, :cells], applied[:, cells:]
    plus = jnp.concatenate([real[:, :half] + real[:, half:], imag[:, :half] + imag[:, half:]], axis=1).astype(BF16)
    minus = jnp.concatenate([real[:, :half] - real[:, half:], imag[:, :half] - imag[:, half:]], axis=1).astype(BF16)
    even = jnp.dot(plus, right[0], preferred_element_type=F32)
    odd = jnp.dot(minus, right[1], preferred_element_type=F32)
    low = (even + odd).astype(BF16).astype(F32)
    high = (even - odd).astype(BF16).astype(F32)

    def fold(part, sign):
        top, bottom = part[:half], part[half:]
        both = (top + sign * bottom).astype(BF16)
        return jnp.concatenate([both[:, :half], both[:, half:]], axis=0)

    sums = jnp.concatenate([fold(low, 1.0), fold(high, 1.0)], axis=1)
    diffs = jnp.concatenate([fold(low, -1.0), fold(high, -1.0)], axis=1)
    even = jnp.dot(left[0], sums, preferred_element_type=F32)
    odd = jnp.dot(left[1], diffs, preferred_element_type=F32)
    top = even + odd
    bottom = even - odd
    arr_real = jnp.concatenate([top[:half], bottom[:half]], axis=0)
    arr_imag = jnp.concatenate([top[half:], bottom[half:]], axis=0)
    back = back_second[0].astype(F32)
    back_real, back_imag = back[:, :cells], back[:, cells:]
    product = jnp.concatenate(
        [back_real * arr_real + back_imag * arr_imag, back_imag * arr_real - back_real * arr_imag], axis=1
    )
    mask_second = soften(reduce_rows(product) * scale_all)
    return (mask_first, mask_second)


def solution(mesh):
    fine = Mesh(mesh.devices.reshape(2, 4, 2, 4, 2), AXES)
    placed = (P(AXES, None), P(AXES, None, None), P(AXES, None, None))
    return jax.shard_map(
        body, mesh=fine, in_specs=placed, out_specs=(P(AXES, None), P(AXES, None)), check_vma=False
    )
```

time: 947 us -> 174 us (0.18)
  waiting for transfers between devices: 773 us -> 9.04 us
  blocking collectives: 0 us -> 110 us
  other arithmetic: 72.5 us -> 25.5 us
  matrix products: 59.2 us -> 14.2 us
  local copies, waits for them, and re-layouts: 20.4 us -> 8.96 us
  between operations: 14.4 us -> 4.82 us
    reduce_scatter x1 -> x0, waiting for transfers between devices: 657 us -> none  [body(): lax.psum_scatter(intersection_conj(back_rows, arrived, cells), ('mgroup',...]
    psum x1 -> x0, waiting for transfers between devices: 116 us -> none  [body(): summed = lax.psum(intersection_first(back_rows, fields), ('mgroup', 'msub'))]
    all_to_all x0 -> x3, blocking collectives: none -> 110 us  [the longest x2 76.4 us: reduce_rows(): parts = lax.all_to_all(both, PEERS, 0, 0, tiled=True)]
    dot_general x5 -> x6, matrix products: 59.2 us -> 14.2 us  [the longest x2 6.9 us: body(): even = jnp.dot(plus, right[0], preferred_element_type=F32)]
    neg x2 -> x0, other arithmetic: 19.4 us -> none  [the longest x1 16.7 us: body(): -chirp_imag]
    convert_element_type x4 -> x8, other arithmetic: 25.5 us -> 12 us  [the longest x2 4.26 us: reduce_rows(): both = (keep.astype(F32) + swap_cores(away).astype(F32)).astype(BF16)]
    unnamed x10 -> x14, local copies, waits for them, and re-layouts: 17.4 us -> 4.51 us
  transfers between devices with their start and end apart: 2 -> 3, of which waited for: 2 -> 3; matrix products, arithmetic and copies ran while one was open for 5% -> 2% of each run, Pallas kernels for 0% -> 0%
where the time goes in v1:
time: 174 us; the launch traced here: 173 us
  blocking collectives  110 us (63%)
  other arithmetic  25.5 us (15%)
  matrix products  14.2 us (8%)
  waiting for transfers between devices  9.04 us (5%)
  local copies, waits for them, and re-layouts  8.96 us (5%)
  between operations  4.82 us (3%)
    all_to_all x2, blocking collectives, reduce_rows(): parts = lax.all_to_all(both, PEERS, 0, 0, tiled=True)  76.4 us
    all_to_all x1, blocking collectives, gather_rows(): lax.all_to_all(jnp.broadcast_to(own[None], (64, rows, width)), PEERS, 0,...  33.9 us
    ppermute x3, waiting for transfers between devices, swap_cores(): return lax.ppermute(block, 'core', [(0, 1), (1, 0)])  9.04 us
    dot_general x2, matrix products, body(): even = jnp.dot(plus, right[0], preferred_element_type=F32)  6.9 us
    unnamed x14, local copies, waits for them, and re-layouts  4.51 us
    convert_element_type x2, other arithmetic, reduce_rows(): both = (keep.astype(F32) + swap_cores(away).astype(F32)).astype(BF16)  4.26 us
    add x1, other arithmetic, body(): back_real * arr_real + back_imag * arr_imag  3.73 us
  transfers between devices with their start and end apart: 3, of which 3 were waited for; matrix products, arithmetic and copies ran while one was open for 2% of the time, Pallas kernels for 0%

profile of v1, /device:TPU:0, one launch (start us, length us, event | category | flops | bytes accessed | tf_op | source)
XLA Modules:
  0.0 173.1 jit_solution(1536841641953135454)
XLA Ops:
  0.6 1.3 fusion.43
  5.8 0.8 constant_dynamic-slice_fusion.1
  7.0 3.2 %convert_multiply_fusion.1 = f32[8,2,64,2048]{3,2,1,0:T(8,128)S(1)} fusion(bf16[8,2,64,2048]{3,2,1,0:T(8,128)(2,1)} %bitcast.49, bf16[8,2,64,1024]{3,2,1,0:T(8,128)(2,1)S(1)} %multiply_convert_fusion.1), kind=kLoop, calls=%fused_computation.3 | loop fusion | flops 12582912 | bytes 14680064 | tf_op jit(solution)/shard_map/mul | solution.py:96
  10.2 3.2 %copy-done = f32[8,2,64,2048]{3,2,1,0:T(8,128)} copy-done((f32[8,2,64,2048]{3,2,1,0:T(8,128)}, f32[8,2,64,2048]{3,2,1,0:T(8,128)S(1)}, u32[]{:S(2)}) %copy-start) | copy-done | bytes 8388632
  13.8 4.3 %collective-permute-done = bf16[8,64,2048]{2,1,0:T(8,128)(2,1)} collective-permute-done((bf16[8,64,2048]{2,1,0:T(8,128)(2,1)S(1)}, bf16[8,64,2048]{2,1,0:T(8,128)(2,1)}, u32[]{:S(2)}, u32[]{:S(2)}) %collective-permute-start) | collective-permute-done | bytes 2097184 | tf_op jit(solution)/shard_map/ppermute | solution.py:61
  18.1 3.5 %fusion.3 = bf16[8,64,2048]{2,1,0:T(8,128)(2,1)S(1)} fusion(bf16[8,64,2048]{2,1,0:T(8,128)(2,1)} %collective-permute-done, f32[8,2,64,2048]{3,2,1,0:T(8,128)} %copy-done, s32[]{:T(128)S(6)} %select_n.30), kind=kLoop, calls=%fused_computation.12 | loop fusion | flops 3145728 | bytes 8388612 | tf_op jit(solution)/shard_map/convert_element_type | solution.py:70
  21.6 40.9 %all_to_all.15 = bf16[64,8,2048]{2,1,0:T(8,128)(2,1)S(1)} all-to-all(bf16[64,8,2048]{2,1,0:T(8,128)(2,1)S(1)} %bitcast.48), channel_id=1, replica_groups=mesh['yh'=2,'z'=4,'core'=2,'x'=4,'yl'=2] {'yh','z','x','yl'}, dimensions={0} | all-to-all | bytes 4194304 | tf_op jit(solution)/shard_map/all_to_all | solution.py:72
  63.7 33.9 %all_to_all.16 = bf16[64,8,2048]{2,1,0:T(8,128)(2,1)S(1)} all-to-all(bf16[64,8,2048]{2,1,0:T(8,128)(2,1)S(1)} %broadcast_in_dim.2), channel_id=1, replica_groups=mesh['yh'=2,'z'=4,'core'=2,'x'=4,'yl'=2] {'yh','z','x','yl'}, dimensions={0} | all-to-all | bytes 4194304 | tf_op jit(solution)/shard_map/all_to_all | solution.py:79
  98.0 3.2 %bitcast_convert_fusion = f32[1024,2048]{1,0:T(8,128)S(1)} fusion(bf16[1,1024,2048]{2,1,0:T(8,128)(2,1)} %param.10), kind=kLoop, calls=%fused_computation.10 | loop fusion | flops 2097152 | bytes 12582912 | tf_op jit(solution)/shard_map/convert_element_type | solution.py:127
  102.0 1.9 %select_bitcast_fusion.1 = (bf16[8,1,64,2048]{3,2,1,0:T(8,128)(2,1)S(1)}, bf16[8,1,64,2048]{3,2,1,0:T(8,128)(2,1)S(1)}) fusion(bf16[8,64,2048]{2,1,0:T(8,128)(2,1)} %collective-permute-done.1, pred[]{:T(512)S(6)} %eq.4, bf16[8,64,2048]{2,1,0:T(8,128)(2,1)S(1)} %bitcast.46), kind=kLoop, calls=%fused_computation.54 | loop fusion | flops 2097152 | bytes 8388609 | tf_op jit(solution)/shard_map/stack | solution.py:84
  104.2 2.0 %fusion.1 = f32[1024,2048]{1,0:T(8,128)S(1)} fusion(bf16[1024,1024]{1,0:T(8,128)(2,1)S(1)} %multiply_convert_fusion, bf16[8,2,64,2048]{3,2,1,0:T(8,128)(2,1)S(1)} %pad_maximum_fusion.1), kind=kLoop, calls=%fused_computation.4 | loop fusion | flops 16777216 | bytes 14680064 | tf_op jit(solution)/shard_map/convert_element_type | solution.py:105
  106.3 3.2 %fusion.24 = f32[1024,1024]{1,0:T(8,128)} fusion(bf16[512,1024]{1,0:T(8,128)(2,1)S(1)} %copy-done.6, f32[1024,2048]{1,0:T(8,128)S(1)} %fusion.1), kind=kOutput, calls=%fused_computation.55 | convolution fusion | flops 1074790400 | bytes 9437184 | tf_op jit(solution)/shard_map/dot_general | solution.py:109
  109.5 1.3 fusion.25
  110.8 1.3 convolution_add_fusion
  112.1 3.7 %fusion.5 = (f32[1024,1024]{1,0:T(8,128)S(1)}, f32[1024,1024]{1,0:T(8,128)S(1)}) fusion(f32[1024,1024]{1,0:T(8,128)S(1)} %convolution_add_fusion, f32[1024,1024]{1,0:T(8,128)} %fusion.24, bf16[512,1024]{1,0:T(8,128)(2,1)S(1)} %copy-done.1, f32[1024,2048]{1,0:T(8,128)S(1)} %fusion.1), kind=kOutput, calls=%fused_computation.26 | convolution fusion | flops 1082130432 | bytes 22020096 | tf_op jit(solution)/shard_map/dot_general | solution.py:109
  115.8 1.2 add_convert_fusion.1
  117.4 1.3 copy-done.4
  118.6 2.3 %fusion.16 = f32[1024,1024]{1,0:T(8,128)S(1)} fusion(bf16[1024,1024]{1,0:T(8,128)(2,1)S(1)} %copy-done.4, bf16[512,512]{1,0:T(8,128)(2,1)S(1)} %get-tuple-element.23, bf16[512,512]{1,0:T(8,128)(2,1)S(1)} %get-tuple-element.22, bf16[512,512]{1,0:T(8,128)(2,1)S(1)} %get-tuple-element.21, bf16[512,512]{1,0:T(8,128)(2,1)S(1)} %get-tuple-element.20), kind=kOutput, calls=%fused_computation.37 | convolution fusion | flops 2155872256 | bytes 8388608 | tf_op jit(solution)/shard_map/dot_general | solution.py:122
  121.0 2.4 %fusion.36 = (f32[1024,1024]{1,0:T(8,128)S(1)}, f32[1024,1024]{1,0:T(8,128)S(1)}) fusion(f32[1024,1024]{1,0:T(8,128)S(1)} %fusion.16, bf16[1024,1024]{1,0:T(8,128)(2,1)S(1)} %copy-done.3, bf16[512,512]{1,0:T(8,128)(2,1)S(1)} %get-tuple-element.27, bf16[512,512]{1,0:T(8,128)(2,1)S(1)} %get-tuple-element.26, bf16[512,512]{1,0:T(8,128)(2,1)S(1)} %get-tuple-element.25, ...), kind=kOutput, calls=%fused_computation.77 | convolution fusion | flops 2157969408 | bytes 16777216 | tf_op jit(solution)/shard_map/dot_general | solution.py:121
  124.5 3.7 %multiply_add_fusion = (f32[1024,1024]{1,0:T(8,128)S(1)}, f32[1024,1024]{1,0:T(8,128)}) fusion(f32[1024,2048]{1,0:T(8,128)S(1)} %bitcast_convert_fusion, f32[512,1024]{1,0:T(8,128)S(1)} %get-tuple-element.13, f32[512,1024]{1,0:T(8,128)S(1)} %get-tuple-element.11, f32[512,1024]{1,0:T(8,128)S(1)} %get-tuple-element.12, f32[512,1024]{1,0:T(8,128)S(1)} %get-tuple-element.10), kind=kLoop, calls=%fused_computation.16 | loop fusion | flops 8388608 | bytes 25165824 | tf_op jit(solution)/shard_map/add | solution.py:130
  128.2 3.0 %pad_maximum_fusion = f32[1024,2048]{1,0:T(8,128)S(1)} fusion(f32[1024,1024]{1,0:T(8,128)} %get-tuple-element.5, f32[1024,1024]{1,0:T(8,128)S(1)} %get-tuple-element.4), kind=kLoop, calls=%fused_computation | loop fusion | flops 2097152 | bytes 16777216 | tf_op jit(solution)/shard_map/concatenate | solution.py:129
  131.8 4.0 %collective-permute-done.2 = bf16[8,64,2048]{2,1,0:T(8,128)(2,1)S(1)} collective-permute-done((bf16[8,64,2048]{2,1,0:T(8,128)(2,1)S(1)}, bf16[8,64,2048]{2,1,0:T(8,128)(2,1)S(1)}, u32[]{:S(2)}, u32[]{:S(2)}) %collective-permute-start.2) | collective-permute-done | bytes 2097184 | tf_op jit(solution)/shard_map/ppermute | solution.py:61
  135.8 0.8 fusion.2
  136.6 35.5 %all_to_all.17 = bf16[64,8,2048]{2,1,0:T(8,128)(2,1)S(1)} all-to-all(bf16[64,8,2048]{2,1,0:T(8,128)(2,1)S(1)} %bitcast.47), channel_id=1, replica_groups=mesh['yh'=2,'z'=4,'core'=2,'x'=4,'yl'=2] {'yh','z','x','yl'}, dimensions={0} | all-to-all | bytes 4194304 | tf_op jit(solution)/shard_map/all_to_all | solution.py:72
  (37 shorter events, 6.3 us)
Async XLA Ops:
  10.2 3.2 %copy-start = (f32[8,2,64,2048]{3,2,1,0:T(8,128)}, f32[8,2,64,2048]{3,2,1,0:T(8,128)S(1)}, u32[]{:S(2)}) copy-start(f32[8,2,64,2048]{3,2,1,0:T(8,128)S(1)} %convert_multiply_fusion.1) | copy-start | bytes 25165828
  13.7 4.4 %collective-permute-start = (bf16[8,64,2048]{2,1,0:T(8,128)(2,1)S(1)}, bf16[8,64,2048]{2,1,0:T(8,128)(2,1)}, u32[]{:S(2)}, u32[]{:S(2)}) collective-permute-start(bf16[8,64,2048]{2,1,0:T(8,128)(2,1)S(1)} %fusion.4), channel_id=1, source_target_pairs={{0,8},{8,0},{1,9},{9,1},{2,10},{10,2},{3,11},{11,3},{4,12},{12,4},... | collective-permute-start | bytes 6291464 | tf_op jit(solution)/shard_map/ppermute | solution.py:61
  97.7 4.3 %collective-permute-start.1 = (bf16[8,64,2048]{2,1,0:T(8,128)(2,1)S(1)}, bf16[8,64,2048]{2,1,0:T(8,128)(2,1)}, u32[]{:S(2)}, u32[]{:S(2)}) collective-permute-start(bf16[8,64,2048]{2,1,0:T(8,128)(2,1)S(1)} %bitcast.45), channel_id=1, source_target_pairs={{0,8},{8,0},{1,9},{9,1},{2,10},{10,2},{3,11},{11,3},{4,12},{12,4},... | collective-permute-start | bytes 6291464 | tf_op jit(solution)/shard_map/ppermute | solution.py:61
  104.2 2.0 %copy-start.6 = (bf16[512,1024]{1,0:T(8,128)(2,1)S(1)}, bf16[512,1024]{1,0:T(8,128)(2,1)}, u32[]{:S(2)}) copy-start(bf16[512,1024]{1,0:T(8,128)(2,1)} %constant.70) | copy-start | bytes 3145732
  106.3 3.2 %copy-start.5 = (bf16[512,1024]{1,0:T(8,128)(2,1)S(1)}, bf16[512,1024]{1,0:T(8,128)(2,1)}, u32[]{:S(2)}) copy-start(bf16[512,1024]{1,0:T(8,128)(2,1)} %constant.72) | copy-start | bytes 3145732
  109.5 1.3 copy-start.2
  110.8 1.3 copy-start.1
  117.0 1.6 copy-start.4
  118.6 2.3 %copy-start.3 = (bf16[1024,1024]{1,0:T(8,128)(2,1)S(1)}, bf16[1024,1024]{1,0:T(8,128)(2,1)}, u32[]{:S(2)}) copy-start(bf16[1024,1024]{1,0:T(8,128)(2,1)} %constant.59) | copy-start | bytes 6291460
  131.6 4.2 %collective-permute-start.2 = (bf16[8,64,2048]{2,1,0:T(8,128)(2,1)S(1)}, bf16[8,64,2048]{2,1,0:T(8,128)(2,1)S(1)}, u32[]{:S(2)}, u32[]{:S(2)}) collective-permute-start(bf16[8,64,2048]{2,1,0:T(8,128)(2,1)S(1)} %fusion.7), channel_id=1, source_target_pairs={{0,8},{8,0},{1,9},{9,1},{2,10},{10,2},{3,11},{11,3},{4,12},{12,4},... | collective-permute-start | bytes 6291464 | tf_op jit(solution)/shard_map/ppermute | solution.py:61
